TPU v7x, 512 devices: a whole 4x4x16 slice. The times are simulated.
512 devices in a mesh: dfa: 32 (over y, x, z_hi), hid: 16 (over z_lo, core).
Axes of the slice: x: 4, y: 4, z: 16 (z_hi: 2, z_lo: 8; z = z_hi * 8 + z_lo), core: 2. Of those that a mesh axis runs over, the one named last changes fastest.
Arguments:
- beta_last: bfloat16 [256, 32, 16, 64], P('dfa', None, 'hid'), may hold values from -6 to 6
- transition: bfloat16 [32, 16, 64, 32768], P(None, 'hid', None, 'dfa'), may hold values from -0.03125 to 0.03125
- emission: bfloat16 [64, 16, 2048], P(None, 'hid'), may hold values from 0.049804688 to 0.59765625
- successor: int32 [256, 8], replicated, may hold values from 0 to 255
- token_set: int32 [256, 8], replicated, may hold values from 0 to 63
Outputs:
- table: bfloat16 [2, 256, 32, 16, 64], P(None, 'dfa', None, 'hid')
All inputs are finite; a program needn't handle non-finite values.
Results may differ from a plain program's by a relative error of at most 0.0056.
Values may be sent and summed in bfloat16 or wider, within the bound.
No kernel may reach another device: no remote copies, remote signals or barrier semaphores. Data moves between devices by JAX's collectives and lax.ppermute only.
A program may use at most 128 MiB of HBM per device.

v0:
```python
import jax
import jax.numpy as jnp
from jax import lax
from jax.sharding import PartitionSpec as P

POS = 2


def edge_mix(full_cols, emission_rows, succ_rows, set_rows):
    width = full_cols.shape[0]
    count = succ_rows.shape[0]
    nsets = emission_rows.shape[0]
    total = jnp.zeros((width, count), jnp.float32)
    for column in range(succ_rows.shape[1]):
        picked = jnp.take(full_cols, succ_rows[:, column], axis=1)
        one_hot = (
            lax.broadcasted_iota(jnp.int32, (nsets, count), 0) == set_rows[:, column][None, :]
        ).astype(jnp.bfloat16)
        weights = lax.dot_general(
            emission_rows, one_hot, (((0,), (0,)), ((), ())), preferred_element_type=jnp.float32
        )
        total = total + weights * picked.astype(jnp.float32)
    return total.astype(jnp.bfloat16)


def local(beta_last, transition, emission, successor, token_set):
    state_count = beta_last.shape[0]
    block_count = beta_last.shape[1]
    cell_count = beta_last.shape[3]
    width = block_count * cell_count
    beta_cols = beta_last.reshape(state_count, width).T
    trans_block = transition.reshape(width, transition.shape[3])
    emission_rows = emission.reshape(emission.shape[0], width)
    results = []
    for position in range(POS):
        full_cols = lax.all_gather(beta_cols, "dfa", axis=1, tiled=True)
        first_row = lax.axis_index("dfa") * state_count
        succ_own = lax.dynamic_slice_in_dim(successor, first_row, state_count, 0)
        set_own = lax.dynamic_slice_in_dim(token_set, first_row, state_count, 0)
        own_cols = edge_mix(full_cols, emission_rows, succ_own, set_own)
        mixed_cols = lax.all_gather(own_cols, "dfa", axis=1, tiled=True)
        summed = lax.psum_scatter(
            lax.dot_general(
                trans_block,
                mixed_cols,
                (((0,), (0,)), ((), ())),
                preferred_element_type=jnp.float32,
            ),
            "hid",
            scatter_dimension=0,
            tiled=True,
        )
        beta_cols = lax.all_to_all(
            summed.astype(jnp.bfloat16), "dfa", split_axis=1, concat_axis=0, tiled=True
        )
        results = [beta_cols.T.reshape(state_count, block_count, 1, cell_count)] + results
    return jnp.stack(results)


def solution(mesh):
    return jax.shard_map(
        local,
        mesh=mesh,
        in_specs=(
            P("dfa", None, "hid", None),
            P(None, "hid", None, "dfa"),
            P(None, "hid", None),
            P(),
            P(),
        ),
        out_specs=P(None, "dfa", None, "hid", None),
        check_vma=False,
    )
```

profile of v0, /device:TPU:2, one launch (start us, length us, event | category | flops | bytes accessed | tf_op | source)
XLA Modules:
  0.0 713.5 jit_solution(4217858540283520598)
XLA Ops:
  6.5 1.6 reshape.29
  8.2 0.8 constant_dynamic-slice_fusion
  9.2 0.2 convolution_bitcast_fusion.7
  9.4 0.2 convolution_bitcast_fusion.1
  9.6 0.2 convolution_bitcast_fusion.2
  9.8 0.2 convolution_bitcast_fusion.3
  10.0 0.2 convolution_bitcast_fusion.4
  10.2 0.2 convolution_bitcast_fusion.5
  10.4 0.2 convolution_bitcast_fusion.6
  10.7 116.1 %all-gather.5.cloned.1.call-done = bf16[2048,256]{0,1:T(8,128)(2,1)} async-done(((bf16[2048,8]{0,1:T(8,128)(2,1)}), bf16[2048,256]{0,1:T(8,128)(2,1)}) %all-gather.5.cloned.1.call-update) | async-done | bytes 1048592 | tf_op jit(solution)/shard_map/all_gather | solution.py:36
  126.7 2.1 gather_fusion.7
  128.8 0.6 gather_fusion.6
  129.4 0.6 gather_fusion.5
  130.0 0.6 gather_fusion.4
  130.5 0.6 gather_fusion.3
  131.1 0.6 gather_fusion.2
  131.7 0.6 gather_fusion.1
  132.3 0.6 gather_fusion
  132.9 0.8 add_convert_fusion.1
  133.8 100.9 %all-gather.7.cloned.1.call-done = bf16[2048,256]{0,1:T(8,128)(2,1)} async-done(((bf16[2048,8]{0,1:T(8,128)(2,1)}), bf16[2048,256]{0,1:T(8,128)(2,1)}) %all-gather.7.cloned.1.call-update) | async-done | bytes 1048592 | tf_op jit(solution)/shard_map/all_gather | solution.py:41
  234.7 3.8 convolution_bitcast_fusion.9
  238.4 1.3 copy.20
  239.8 96.3 %reduce-scatter.7.cloned.1.call-done = f32[64,256]{1,0:T(8,128)} async-done(((f32[1024,256]{1,0:T(8,128)}), f32[64,256]{1,0:T(8,128)}) %reduce-scatter.7.cloned.1.call-update) | async-done | bytes 65552
  336.1 0.9 copy.21
  337.2 25.9 %all_to_all.38 = bf16[32,2,256]{2,1,0:T(2,128)(2,1)S(1)} all-to-all(bf16[32,2,256]{2,1,0:T(2,128)(2,1)S(1)} %reshape.211), channel_id=1, replica_groups=mesh['dfa'=32,'hid'=16] {'dfa'}, dimensions={0} | all-to-all | bytes 65536 | tf_op jit(solution)/shard_map/all_to_all | solution.py:53
  363.2 0.7 all_to_all.31
  364.0 104.5 %all-gather.9.cloned.1.call-done = bf16[2048,256]{0,1:T(8,128)(2,1)} async-done(((bf16[2048,8]{0,1:T(8,128)(2,1)}), bf16[2048,256]{0,1:T(8,128)(2,1)}) %all-gather.9.cloned.1.call-update) | async-done | bytes 1048592 | tf_op jit(solution)/shard_map/all_gather | solution.py:36
  468.5 2.1 gather_fusion.15
  470.6 0.6 gather_fusion.14
  471.1 0.6 gather_fusion.13
  471.7 0.6 gather_fusion.12
  472.3 0.6 gather_fusion.11
  472.9 0.6 gather_fusion.10
  473.5 0.6 gather_fusion.9
  474.0 0.6 gather_fusion.8
  474.6 0.8 add_convert_fusion
  475.5 100.9 %all-gather.11.cloned.1.call-done = bf16[2048,256]{0,1:T(8,128)(2,1)} async-done(((bf16[2048,8]{0,1:T(8,128)(2,1)}), bf16[2048,256]{0,1:T(8,128)(2,1)}) %all-gather.11.cloned.1.call-update) | async-done | bytes 1048592 | tf_op jit(solution)/shard_map/all_gather | solution.py:41
  576.3 3.8 convolution_bitcast_fusion.8
  580.1 1.3 copy.22
  581.4 96.5 %reduce-scatter.9.cloned.1.call-done = f32[64,256]{1,0:T(8,128)} async-done(((f32[1024,256]{1,0:T(8,128)}), f32[64,256]{1,0:T(8,128)}) %reduce-scatter.9.cloned.1.call-update) | async-done | bytes 65552
  677.9 0.9 copy.23
  678.9 0.7 reshape.213
  679.6 10.2 %all-to-all-start.1 = ((bf16[32,2,256]{2,1,0:T(2,128)(2,1)}), bf16[32,2,256]{2,1,0:T(2,128)(2,1)S(1)}, u32[]{:S(2)}, u32[]{:S(2)}) async-start(bf16[32,2,256]{2,1,0:T(2,128)(2,1)} %reshape.213), calls=%async_computation.1 | async-start | bytes 65536 | tf_op jit(solution)/shard_map/all_to_all | solution.py:53
  689.8 0.1 stack_reshape.7
  690.0 15.6 %all-to-all-done.1 = bf16[32,2,256]{2,1,0:T(2,128)(2,1)S(1)} async-done(((bf16[32,2,256]{2,1,0:T(2,128)(2,1)}), bf16[32,2,256]{2,1,0:T(2,128)(2,1)S(1)}, u32[]{:S(2)}, u32[]{:S(2)}) %all-to-all-start.1) | async-done | bytes 32800 | tf_op jit(solution)/shard_map/all_to_all | solution.py:53
  705.7 0.1 all_to_all.35
  705.9 0.1 stack_reshape.6
  706.0 0.7 pad_maximum_fusion
  (39 shorter events, 0.8 us)
Async XLA Ops:
  6.5 2.6 copy-start
  6.5 120.2 %all-gather.5.cloned.1.call-start = ((), (), s32[]{:S(2)}) async-start(), calls=%async_computation.4 | async-start | bytes 1081344 | tf_op jit(solution)/shard_map/all_gather | solution.py:36
  8.2 226.5 %all-gather.7.cloned.1.call-start = ((), (), s32[]{:S(2)}) async-start(), calls=%async_computation.5 | async-start | bytes 1081344 | tf_op jit(solution)/shard_map/all_gather | solution.py:41
  126.7 2.1 copy-start.1
  133.7 202.3 %reduce-scatter.7.cloned.1.call-start = ((), (), s32[]{:S(2)}) async-start(), calls=%async_computation.8 | async-start | bytes 1114112
  239.8 228.7 %all-gather.9.cloned.1.call-start = ((), (), s32[]{:S(2)}) async-start(), calls=%async_computation.6 | async-start | bytes 1081344 | tf_op jit(solution)/shard_map/all_gather | solution.py:36
  364.0 212.3 %all-gather.11.cloned.1.call-start = ((), (), s32[]{:S(2)}) async-start(), calls=%async_computation.7 | async-start | bytes 1081344 | tf_op jit(solution)/shard_map/all_gather | solution.py:41
  468.5 2.1 copy-start.2
  475.4 214.4 %copy-start.3 = (bf16[2048,8]{0,1:T(8,128)(2,1)S(1)}, bf16[2048,8]{0,1:T(8,128)(2,1)}, u32[]{:S(2)}) copy-start(bf16[2048,8]{0,1:T(8,128)(2,1)} %all_to_all.31) | copy-start | bytes 98308
  475.4 202.5 %reduce-scatter.9.cloned.1.call-start = ((), (), s32[]{:S(2)}) async-start(), calls=%async_computation.9 | async-start | bytes 1114112
  679.6 26.0 %all-to-all-start.1 = ((bf16[32,2,256]{2,1,0:T(2,128)(2,1)}), bf16[32,2,256]{2,1,0:T(2,128)(2,1)S(1)}, u32[]{:S(2)}, u32[]{:S(2)}) async-start(bf16[32,2,256]{2,1,0:T(2,128)(2,1)} %reshape.213), calls=%async_computation.1 | async-start | bytes 65536 | tf_op jit(solution)/shard_map/all_to_all | solution.py:53
Sparse Core Ops, SparseCore 0:
  11.6 115.0 all-gather.4
  133.9 100.7 all-gather.6
  239.9 96.1 reduce-scatter.6
  364.1 104.3 all-gather.8
  475.5 100.7 all-gather.10
  581.6 96.2 reduce-scatter.8
where the time goes:
time: 714 us
  waiting for transfers between devices  631 us (88%)
  blocking collectives  25.9 us (4%)
  local copies, waits for them, and re-layouts  21.4 us (3%)
  between operations  13.8 us (2%)
  starting transfers between devices  10.4 us (1%)
  matrix products  9.82 us (1%)
    all_gather x2, waiting for transfers between devices, local(): full_cols = lax.all_gather(beta_cols, 'dfa', axis=1, tiled=True)  221 us
    all_gather x2, waiting for transfers between devices, local(): mixed_cols = lax.all_gather(own_cols, 'dfa', axis=1, tiled=True)  202 us
    unnamed x8, waiting for transfers between devices  193 us
    all_to_all x1, blocking collectives, local(): lax.all_to_all(summed.astype(jnp.bfloat16), 'dfa', split_axis=1, concat_a...  25.9 us
    all_to_all x1, waiting for transfers between devices, local(): lax.all_to_all(summed.astype(jnp.bfloat16), 'dfa', split_axis=1, concat_a...  15.6 us
  transfers between devices with their start and end apart: 7, of which 7 were waited for; matrix products, arithmetic and copies ran while one was open for 0% of the time, Pallas kernels for 0%

commit v1 on v0

--- a/solution.py
+++ b/solution.py
@@ -33,7 +33,10 @@
     emission_rows = emission.reshape(emission.shape[0], width)
     results = []
     for position in range(POS):
-        full_cols = lax.all_gather(beta_cols, "dfa", axis=1, tiled=True)
+        size = lax.axis_size("dfa")
+        blocks = jnp.stack([beta_cols for _ in range(size)])
+        blocks = lax.all_to_all(blocks, "dfa", split_axis=0, concat_axis=0)
+        full_cols = jnp.concatenate(blocks, axis=1)
         first_row = lax.axis_index("dfa") * state_count
         succ_own = lax.dynamic_slice_in_dim(successor, first_row, state_count, 0)
         set_own = lax.dynamic_slice_in_dim(token_set, first_row, state_count, 0)

time: 714 us -> 611 us (0.86)
  waiting for transfers between devices: 631 us -> 469 us
  blocking collectives: 25.9 us -> 66.6 us
  starting transfers between devices: 10.4 us -> 31.3 us
    all_gather x2 -> x0, waiting for transfers between devices: 221 us -> none  [local(): full_cols = lax.all_gather(beta_cols, 'dfa', axis=1, tiled=True)]
    all_to_all x0 -> x1, blocking collectives: none -> 39.4 us  [local(): blocks = lax.all_to_all(blocks, 'dfa', split_axis=0, concat_axis=0)]
    all_gather x2, waiting for transfers between devices: 202 us -> 232 us  [local(): mixed_cols = lax.all_gather(own_cols, 'dfa', axis=1, tiled=True)]
    all_to_all x0 -> x1, waiting for transfers between devices: none -> 28.2 us  [local(): blocks = lax.all_to_all(blocks, 'dfa', split_axis=0, concat_axis=0)]
    all_to_all x0 -> x1, starting transfers between devices: none -> 20.9 us  [local(): blocks = lax.all_to_all(blocks, 'dfa', split_axis=0, concat_axis=0)]
    unnamed x8 -> x6, waiting for transfers between devices: 193 us -> 193 us
  transfers between devices with their start and end apart: 7 -> 6, of which waited for: 7 -> 6; matrix products, arithmetic and copies ran while one was open for 0% -> 0% of each run, Pallas kernels for 0% -> 0%
where the time goes in v1:
time: 611 us; the launch traced here: 610 us
  waiting for transfers between devices  469 us (77%)
  blocking collectives  66.6 us (11%)
  starting transfers between devices  31.3 us (5%)
  local copies, waits for them, and re-layouts  18.4 us (3%)
  between operations  13.4 us (2%)
  matrix products  9.82 us (2%)
    all_gather x2, waiting for transfers between devices, local(): mixed_cols = lax.all_gather(own_cols, 'dfa', axis=1, tiled=True)  232 us
    unnamed x6, waiting for transfers between devices  193 us
    all_to_all x1, blocking collectives, local(): blocks = lax.all_to_all(blocks, 'dfa', split_axis=0, concat_axis=0)  39.4 us
    all_to_all x1, waiting for transfers between devices, local(): blocks = lax.all_to_all(blocks, 'dfa', split_axis=0, concat_axis=0)  28.2 us
    all_to_all x1, blocking collectives, local(): lax.all_to_all(summed.astype(jnp.bfloat16), 'dfa', split_axis=1, concat_a...  27.2 us
    all_to_all x1, starting transfers between devices, local(): blocks = lax.all_to_all(blocks, 'dfa', split_axis=0, concat_axis=0)  20.9 us
    all_to_all x1, waiting for transfers between devices, local(): lax.all_to_all(summed.astype(jnp.bfloat16), 'dfa', split_axis=1, concat_a...  15.6 us
  transfers between devices with their start and end apart: 6, of which 6 were waited for; matrix products, arithmetic and copies ran while one was open for 0% of the time, Pallas kernels for 0%

profile of v1, /device:TPU:2, one launch (start us, length us, event | category | flops | bytes accessed | tf_op | source)
XLA Modules:
  0.0 610.1 jit_solution(3138104969728397075)
XLA Ops:
  6.5 1.0 reshape.46
  7.5 1.1 stack.8
  8.6 20.9 %all-to-all-start = ((bf16[32,2048,8]{1,2,0:T(8,128)(2,1)}), bf16[32,2048,8]{1,2,0:T(8,128)(2,1)S(1)}, u32[]{:S(2)}, u32[]{:S(2)}) async-start(bf16[32,2048,8]{1,2,0:T(8,128)(2,1)} %stack.8), calls=%async_computation | async-start | bytes 2097152 | tf_op jit(solution)/shard_map/all_to_all | solution.py:38
  29.6 0.8 constant_dynamic-slice_fusion
  30.5 0.2 convolution_bitcast_fusion.1
  30.7 0.2 convolution_bitcast_fusion.2
  30.9 0.2 convolution_bitcast_fusion.3
  31.1 0.2 convolution_bitcast_fusion.4
  31.4 0.2 convolution_bitcast_fusion.5
  31.6 0.2 convolution_bitcast_fusion.6
  31.8 0.2 convolution_bitcast_fusion.7
  32.0 28.2 %all-to-all-done = bf16[32,2048,8]{1,2,0:T(8,128)(2,1)S(1)} async-done(((bf16[32,2048,8]{1,2,0:T(8,128)(2,1)}), bf16[32,2048,8]{1,2,0:T(8,128)(2,1)S(1)}, u32[]{:S(2)}, u32[]{:S(2)}) %all-to-all-start) | async-done | bytes 1048608 | tf_op jit(solution)/shard_map/all_to_all | solution.py:38
  60.2 0.6 gather_fusion
  60.7 0.6 gather_fusion.1
  61.3 0.6 gather_fusion.2
  61.9 0.6 gather_fusion.3
  62.5 0.6 gather_fusion.4
  63.1 0.6 gather_fusion.5
  63.6 0.6 gather_fusion.6
  64.2 0.6 gather_fusion.7
  64.8 0.8 add_convert_fusion.1
  65.7 130.1 %all-gather.3.cloned.1.call-done = bf16[2048,256]{0,1:T(8,128)(2,1)} async-done(((bf16[2048,8]{0,1:T(8,128)(2,1)}), bf16[2048,256]{0,1:T(8,128)(2,1)}) %all-gather.3.cloned.1.call-update) | async-done | bytes 1048592 | tf_op jit(solution)/shard_map/all_gather | solution.py:44
  195.8 3.8 convolution_bitcast_fusion.9
  199.6 1.3 copy.14
  201.0 96.2 %reduce-scatter.7.cloned.1.call-done = f32[64,256]{1,0:T(8,128)} async-done(((f32[1024,256]{1,0:T(8,128)}), f32[64,256]{1,0:T(8,128)}) %reduce-scatter.7.cloned.1.call-update) | async-done | bytes 65552
  297.2 0.9 copy.15
  298.3 27.2 %all_to_all.45 = bf16[32,2,256]{2,1,0:T(2,128)(2,1)S(1)} all-to-all(bf16[32,2,256]{2,1,0:T(2,128)(2,1)S(1)} %reshape.232), channel_id=1, replica_groups=mesh['dfa'=32,'hid'=16] {'dfa'}, dimensions={0} | all-to-all | bytes 65536 | tf_op jit(solution)/shard_map/all_to_all | solution.py:56
  325.7 0.1 stack.9
  325.9 39.4 %all_to_all.46 = bf16[32,2048,8]{1,2,0:T(8,128)(2,1)S(1)} all-to-all(bf16[32,2048,8]{1,2,0:T(8,128)(2,1)S(1)} %stack.10), channel_id=1, replica_groups=mesh['dfa'=32,'hid'=16] {'dfa'}, dimensions={0} | all-to-all | bytes 2097152 | tf_op jit(solution)/shard_map/all_to_all | solution.py:38
  365.3 0.6 gather_fusion.8
  365.9 0.6 gather_fusion.9
  366.5 0.6 gather_fusion.10
  367.1 0.6 gather_fusion.11
  367.6 0.6 gather_fusion.12
  368.2 0.6 gather_fusion.13
  368.8 0.6 gather_fusion.14
  369.4 0.6 gather_fusion.15
  370.0 0.8 add_convert_fusion
  370.8 102.4 %all-gather.5.cloned.1.call-done = bf16[2048,256]{0,1:T(8,128)(2,1)} async-done(((bf16[2048,8]{0,1:T(8,128)(2,1)}), bf16[2048,256]{0,1:T(8,128)(2,1)}) %all-gather.5.cloned.1.call-update) | async-done | bytes 1048592 | tf_op jit(solution)/shard_map/all_gather | solution.py:44
  473.2 3.8 convolution_bitcast_fusion.8
  477.0 1.3 copy.16
  478.3 96.5 %reduce-scatter.9.cloned.1.call-done = f32[64,256]{1,0:T(8,128)} async-done(((f32[1024,256]{1,0:T(8,128)}), f32[64,256]{1,0:T(8,128)}) %reduce-scatter.9.cloned.1.call-update) | async-done | bytes 65552
  574.8 0.9 copy.17
  575.7 0.7 reshape.234
  576.5 10.2 %all-to-all-start.3 = ((bf16[32,2,256]{2,1,0:T(2,128)(2,1)}), bf16[32,2,256]{2,1,0:T(2,128)(2,1)S(1)}, u32[]{:S(2)}, u32[]{:S(2)}) async-start(bf16[32,2,256]{2,1,0:T(2,128)(2,1)} %reshape.234), calls=%async_computation.3 | async-start | bytes 65536 | tf_op jit(solution)/shard_map/all_to_all | solution.py:56
  586.8 15.6 %all-to-all-done.3 = bf16[32,2,256]{2,1,0:T(2,128)(2,1)S(1)} async-done(((bf16[32,2,256]{2,1,0:T(2,128)(2,1)}), bf16[32,2,256]{2,1,0:T(2,128)(2,1)S(1)}, u32[]{:S(2)}, u32[]{:S(2)}) %all-to-all-start.3) | async-done | bytes 32800 | tf_op jit(solution)/shard_map/all_to_all | solution.py:56
  602.6 0.1 all_to_all.40
  602.9 0.7 pad_maximum_fusion
  (32 shorter events, 1.1 us)
Async XLA Ops:
  6.5 24.0 %copy-start = (bf16[64,1,2048]{2,0,1:T(8,128)(2,1)S(1)}, bf16[64,1,2048]{2,0,1:T(8,128)(2,1)}, u32[]{:S(2)}) copy-start(bf16[64,1,2048]{2,0,1:T(8,128)(2,1)} %param.9) | copy-start | bytes 786436
  8.6 51.5 %all-to-all-start = ((bf16[32,2048,8]{1,2,0:T(8,128)(2,1)}), bf16[32,2048,8]{1,2,0:T(8,128)(2,1)S(1)}, u32[]{:S(2)}, u32[]{:S(2)}) async-start(bf16[32,2048,8]{1,2,0:T(8,128)(2,1)} %stack.8), calls=%async_computation | async-start | bytes 2097152 | tf_op jit(solution)/shard_map/all_to_all | solution.py:38
  29.5 166.3 %all-gather.3.cloned.1.call-start = ((), (), s32[]{:S(2)}) async-start(), calls=%async_computation.6 | async-start | bytes 1081344 | tf_op jit(solution)/shard_map/all_gather | solution.py:44
  65.7 231.5 %reduce-scatter.7.cloned.1.call-start = ((), (), s32[]{:S(2)}) async-start(), calls=%async_computation.8 | async-start | bytes 1114112
  200.9 272.3 %all-gather.5.cloned.1.call-start = ((), (), s32[]{:S(2)}) async-start(), calls=%async_computation.7 | async-start | bytes 1081344 | tf_op jit(solution)/shard_map/all_gather | solution.py:44
  370.8 204.0 %reduce-scatter.9.cloned.1.call-start = ((), (), s32[]{:S(2)}) async-start(), calls=%async_computation.9 | async-start | bytes 1114112
  576.5 26.0 %all-to-all-start.3 = ((bf16[32,2,256]{2,1,0:T(2,128)(2,1)}), bf16[32,2,256]{2,1,0:T(2,128)(2,1)S(1)}, u32[]{:S(2)}, u32[]{:S(2)}) async-start(bf16[32,2,256]{2,1,0:T(2,128)(2,1)} %reshape.234), calls=%async_computation.3 | async-start | bytes 65536 | tf_op jit(solution)/shard_map/all_to_all | solution.py:56
Sparse Core Ops, SparseCore 0:
  65.8 129.9 all-gather.2
  201.0 96.1 reduce-scatter.6
  370.9 102.2 all-gather.4
  478.4 96.2 reduce-scatter.8
